TPU v7x, 256 devices: a whole 4x4x8 slice. The times are simulated.
256 devices in a mesh: section: 4 (over x), tp: 64 (over y, z, core).
Axes of the slice: x: 4, y: 4, z: 8, core: 2. Of those that a mesh axis runs over, the one named last changes fastest.
Arguments:
- tokens: bfloat16 [64, 8192], P(None, 'tp'), may hold values from -6 to 6
- norm_gain: float32 [4, 8192], P('section'), may hold values from 0.1 to 1.9
- gate_weight: bfloat16 [4, 8192, 16384], P('section', None, 'tp'), may hold values from -0.09375 to 0.09375
- up_weight: bfloat16 [4, 8192, 16384], P('section', None, 'tp'), may hold values from -0.09375 to 0.09375
- gate_mask: int32 [4, 128, 256], P('section', None, 'tp'), may hold values 0 or 1
- up_mask: int32 [4, 128, 256], P('section', None, 'tp'), may hold values 0 or 1
- down_weight: bfloat16 [4, 16384, 8192], P('section', 'tp'), may hold values from -0.125 to 0.125
- down_mask: int32 [4, 256, 128], P('section', 'tp'), may hold values 0 or 1
- slot_order: int32 [4, 256], P('section', 'tp'), may hold values from 0 to 255, as said below
Outputs:
- received: bfloat16 [4, 64, 8192], P('section', None, 'tp')
Inputs may be any that keep to these rules, and one draw needn't show every extreme that they name: `slot_order`: for each section a permutation of the 256 hidden blocks. Slot k lies on tp device k // 4; block b is computed on tp device b // 4. The slots of tp device t take exactly 1 block from each of the tp devices t, t + 1, ..., t + 4 - 1 (mod 64) and none from others. `gate_mask`: 1 keeps a block, 0 prunes it. `up_mask`: 1 keeps a block, 0 prunes it. `down_mask`: 1 keeps a block, 0 prunes it.
All inputs are finite; a program needn't handle non-finite values.
Results may differ from a plain program's by a relative error of at most 0.014.
Values may be sent and summed in bfloat16 or wider, within the bound.
A program may use at most 128 MiB of HBM per device.

v0:
```python
import jax
import jax.numpy as jnp
from jax import lax
from jax.sharding import PartitionSpec as P


def passed_along(block, axis, distance):
    devices = range(lax.axis_size(axis))
    route = [((i - distance) % len(devices), i) for i in devices]
    return lax.ppermute(block, axis, route)


def expand_mask(mask, width):
    return jnp.repeat(jnp.repeat(mask, width, axis=0), width, axis=1)


def masked(weight, mask, width):
    return weight * expand_mask(mask, width).astype(jnp.bfloat16)


def body(
    tokens,
    norm_gain,
    gate_weight,
    up_weight,
    gate_mask,
    up_mask,
    down_weight,
    down_mask,
    slot_order,
):
    sections = lax.axis_size("section")
    tp_count = lax.axis_size("tp")
    section_pos = lax.axis_index("section")
    tp_pos = lax.axis_index("tp")
    width = gate_weight.shape[1] // gate_mask.shape[1]
    w_gate = masked(gate_weight[0], gate_mask[0], width)
    w_up = masked(up_weight[0], up_mask[0], width)
    w_down = masked(down_weight[0], down_mask[0], width)
    gain = norm_gain[0]
    my_blocks = slot_order[0]
    per_device = my_blocks.shape[0]
    row_count, own_cols = tokens.shape
    window = min(tp_count, per_device)
    capacity = per_device // window
    slot_ids = jnp.arange(capacity, dtype=jnp.int32)
    my_source = my_blocks // per_device
    my_offset = (my_source - tp_pos) % tp_count
    lanes = jnp.arange(per_device, dtype=jnp.int32)
    earlier = (my_source[None, :] == my_source[:, None]) & (lanes[None, :] < lanes[:, None])
    my_rank = jnp.sum(earlier.astype(jnp.int32), axis=1)
    send_lists = []
    for offset in range(window):
        if offset == 0:
            table_row = my_blocks
        else:
            table_row = passed_along(my_blocks, "tp", offset)
        row_source = table_row // per_device
        row_block = table_row % per_device
        from_me = (row_source == tp_pos).astype(jnp.int32)
        order_rank = jnp.cumsum(from_me) - 1
        picks = (from_me[None, :] == 1) & (order_rank[None, :] == slot_ids[:, None])
        send_lists.append(jnp.sum(jnp.where(picks, row_block[None, :], 0), axis=1))
    x_full = lax.all_gather(tokens, "tp", axis=1, tiled=True)
    saved = jnp.zeros((row_count, own_cols), jnp.bfloat16)
    for round_pos in range(sections):
        x_own = lax.dynamic_slice_in_dim(x_full, tp_pos * own_cols, own_cols, 1)
        widened = x_full.astype(jnp.float32)
        scale = lax.rsqrt(jnp.mean(widened * widened, axis=-1, keepdims=True) + 1e-05)
        normed = (widened * scale * gain).astype(jnp.bfloat16)
        gate = jnp.dot(normed, w_gate, preferred_element_type=jnp.float32)
        upper = jnp.dot(normed, w_up, preferred_element_type=jnp.float32)
        hidden = (jax.nn.silu(gate) * upper).astype(jnp.bfloat16)
        flat = (
            hidden.reshape(row_count, per_device, width)
            .transpose(1, 0, 2)
            .reshape(per_device, row_count * width)
        )
        arrivals = []
        for gather_offset in range(window):
            outgoing = flat[send_lists[gather_offset]]
            if gather_offset == 0:
                arrivals.append(outgoing)
            else:
                arrivals.append(passed_along(outgoing, "tp", tp_count - gather_offset))
        stacked = jnp.stack(arrivals)
        chosen = stacked[my_offset, my_rank]
        mine = (
            chosen.reshape(per_device, row_count, width)
            .transpose(1, 0, 2)
            .reshape(row_count, per_device * width)
        )
        partial_sum = jnp.dot(mine, w_down, preferred_element_type=jnp.float32)
        summed = lax.psum_scatter(partial_sum, "tp", scatter_dimension=1, tiled=True)
        y_own = (x_own.astype(jnp.float32) + summed).astype(jnp.bfloat16)
        section_full = lax.all_gather(y_own, "tp", axis=1, tiled=True)
        x_full = passed_along(section_full, "section", 1)
        got_own = lax.dynamic_slice_in_dim(x_full, tp_pos * own_cols, own_cols, 1)
        saved = jnp.where(section_pos == (round_pos + 1) % sections, got_own, saved)
    return saved[None]


def solution(mesh):
    return jax.shard_map(
        body,
        mesh=mesh,
        in_specs=(
            P(None, "tp"),
            P("section", None),
            P("section", None, "tp"),
            P("section", None, "tp"),
            P("section", None, "tp"),
            P("section", None, "tp"),
            P("section", "tp", None),
            P("section", "tp", None),
            P("section", "tp"),
        ),
        out_specs=P("section", None, "tp"),
        check_vma=False,
    )
```

profile of v0, /device:TPU:1, one launch (start us, length us, event | category | flops | bytes accessed | tf_op | source)
XLA Modules:
  0.0 1125.9 jit_solution(15061843299415078217)
XLA Ops:
  16.4 6.4 copy.36
  23.1 6.4 copy.37
  30.5 4.6 bitcast_multiply_fusion.2
  46.1 38.5 %all-gather.6.cloned.1.call-done = bf16[64,8192]{1,0:T(8,128)(2,1)} async-done(((bf16[64,128]{1,0:T(8,128)(2,1)}), bf16[64,8192]{1,0:T(8,128)(2,1)}) %all-gather.6.cloned.1.call-update) | async-done | bytes 1048592 | tf_op jit(solution)/shard_map/all_gather | solution.py:64
  98.5 6.4 copy.41
  105.0 4.4 bitcast_multiply_fusion
  110.6 4.9 fusion.6
  115.6 130.5 %reduce-scatter.5.cloned.1.call-done = f32[64,128]{1,0:T(8,128)} async-done(((f32[64,8192]{1,0:T(8,128)}), f32[64,128]{1,0:T(8,128)}) %reduce-scatter.5.cloned.1.call-update) | async-done | bytes 32784 | tf_op jit(solution)/shard_map/reduce_scatter | solution.py:94
  247.5 76.0 %all-gather.8.cloned.1.call-done = bf16[64,8192]{1,0:T(8,128)(2,1)} async-done(((bf16[64,128]{1,0:T(8,128)(2,1)}), bf16[64,8192]{1,0:T(8,128)(2,1)}) %all-gather.8.cloned.1.call-update) | async-done | bytes 1048592 | tf_op jit(solution)/shard_map/all_gather | solution.py:96
  324.5 24.8 %collective-permute-done.6 = bf16[64,8192]{1,0:T(8,128)(2,1)S(1)} collective-permute-done((bf16[64,8192]{1,0:T(8,128)(2,1)}, bf16[64,8192]{1,0:T(8,128)(2,1)S(1)}, u32[]{:S(2)}, u32[]{:S(2)}) %collective-permute-start.6) | collective-permute-done | bytes 1048608 | tf_op jit(solution)/shard_map/ppermute | solution.py:10
  365.8 4.9 fusion.4
  370.8 132.0 %reduce-scatter.7.cloned.1.call-done = f32[64,128]{1,0:T(8,128)} async-done(((f32[64,8192]{1,0:T(8,128)}), f32[64,128]{1,0:T(8,128)}) %reduce-scatter.7.cloned.1.call-update) | async-done | bytes 32784 | tf_op jit(solution)/shard_map/reduce_scatter | solution.py:94
  504.2 75.2 %all-gather.10.cloned.1.call-done = bf16[64,8192]{1,0:T(8,128)(2,1)} async-done(((bf16[64,128]{1,0:T(8,128)(2,1)}), bf16[64,8192]{1,0:T(8,128)(2,1)}) %all-gather.10.cloned.1.call-update) | async-done | bytes 1048592 | tf_op jit(solution)/shard_map/all_gather | solution.py:96
  580.5 24.8 %collective-permute-done.10 = bf16[64,8192]{1,0:T(8,128)(2,1)S(1)} collective-permute-done((bf16[64,8192]{1,0:T(8,128)(2,1)}, bf16[64,8192]{1,0:T(8,128)(2,1)S(1)}, u32[]{:S(2)}, u32[]{:S(2)}) %collective-permute-start.10) | collective-permute-done | bytes 1048608 | tf_op jit(solution)/shard_map/ppermute | solution.py:10
  612.3 4.3 collective-permute-start.12
  621.8 4.9 fusion.2
  626.8 132.0 %reduce-scatter.9.cloned.1.call-done = f32[64,128]{1,0:T(8,128)} async-done(((f32[64,8192]{1,0:T(8,128)}), f32[64,128]{1,0:T(8,128)}) %reduce-scatter.9.cloned.1.call-update) | async-done | bytes 32784 | tf_op jit(solution)/shard_map/reduce_scatter | solution.py:94
  760.2 75.6 %all-gather.12.cloned.1.call-done = bf16[64,8192]{1,0:T(8,128)(2,1)} async-done(((bf16[64,128]{1,0:T(8,128)(2,1)}), bf16[64,8192]{1,0:T(8,128)(2,1)}) %all-gather.12.cloned.1.call-update) | async-done | bytes 1048592 | tf_op jit(solution)/shard_map/all_gather | solution.py:96
  837.0 24.8 %collective-permute-done.14 = bf16[64,8192]{1,0:T(8,128)(2,1)S(1)} collective-permute-done((bf16[64,8192]{1,0:T(8,128)(2,1)}, bf16[64,8192]{1,0:T(8,128)(2,1)S(1)}, u32[]{:S(2)}, u32[]{:S(2)}) %collective-permute-start.14) | collective-permute-done | bytes 1048608 | tf_op jit(solution)/shard_map/ppermute | solution.py:10
  868.8 4.3 collective-permute-start.16
  878.2 4.9 fusion
  883.2 132.0 %reduce-scatter.11.cloned.1.call-done = f32[64,128]{1,0:T(8,128)} async-done(((f32[64,8192]{1,0:T(8,128)}), f32[64,128]{1,0:T(8,128)}) %reduce-scatter.11.cloned.1.call-update) | async-done | bytes 32784 | tf_op jit(solution)/shard_map/reduce_scatter | solution.py:94
  1016.6 75.4 %all-gather.14.cloned.1.call-done = bf16[64,8192]{1,0:T(8,128)(2,1)} async-done(((bf16[64,128]{1,0:T(8,128)(2,1)}), bf16[64,8192]{1,0:T(8,128)(2,1)}) %all-gather.14.cloned.1.call-update) | async-done | bytes 1048592 | tf_op jit(solution)/shard_map/all_gather | solution.py:96
  1093.1 24.9 %collective-permute-done.18 = bf16[64,8192]{1,0:T(8,128)(2,1)} collective-permute-done((bf16[64,8192]{1,0:T(8,128)(2,1)}, bf16[64,8192]{1,0:T(8,128)(2,1)}, u32[]{:S(2)}, u32[]{:S(2)}) %collective-permute-start.18) | collective-permute-done | bytes 1048608 | tf_op jit(solution)/shard_map/ppermute | solution.py:10
  (154 shorter events, 81.4 us)
Async XLA Ops:
  6.5 78.0 %all-gather.6.cloned.1.call-start = ((), (), s32[]{:S(2)}) async-start(), calls=%async_computation.4 | async-start | bytes 1064960 | tf_op jit(solution)/shard_map/all_gather | solution.py:64
  6.5 31.1 %collective-permute-start = (s32[4]{0:T(128)}, s32[4]{0:T(128)S(1)}, u32[]{:S(2)}, u32[]{:S(2)}) collective-permute-start(s32[4]{0:T(128)} %bitcast.171), channel_id=1, source_target_pairs={{63,0},{0,1},{1,2},{2,3},{3,4},{4,5},{5,6},{6,7},{7,8},{8,9},{9,10... | collective-permute-start | bytes 56 | tf_op jit(solution)/shard_map/ppermute | solution.py:10
  9.6 30.2 %collective-permute-start.2 = (s32[4]{0:T(128)}, s32[4]{0:T(128)S(1)}, u32[]{:S(2)}, u32[]{:S(2)}) collective-permute-start(s32[4]{0:T(128)} %bitcast.172), channel_id=1, source_target_pairs={{62,0},{63,1},{0,2},{1,3},{2,4},{3,5},{4,6},{5,7},{6,8},{7,9},{8,1... | collective-permute-start | bytes 56 | tf_op jit(solution)/shard_map/ppermute | solution.py:10
  11.2 30.8 %collective-permute-start.4 = (s32[4]{0:T(128)}, s32[4]{0:T(128)S(1)}, u32[]{:S(2)}, u32[]{:S(2)}) collective-permute-start(s32[4]{0:T(128)} %bitcast.173), channel_id=1, source_target_pairs={{61,0},{62,1},{63,2},{0,3},{1,4},{2,5},{3,6},{4,7},{5,8},{6,9},{7,... | collective-permute-start | bytes 56 | tf_op jit(solution)/shard_map/ppermute | solution.py:10
  12.9 233.1 %reduce-scatter.5.cloned.1.call-start = ((), (), s32[]{:S(2)}) async-start(), calls=%async_computation.5 | async-start | bytes 2129920 | tf_op jit(solution)/shard_map/reduce_scatter | solution.py:94
  92.0 17.5 %collective-permute-start.1 = (bf16[1,4096]{1,0:T(2,128)(2,1)S(1)}, bf16[1,4096]{1,0:T(2,128)(2,1)S(1)}, u32[]{:S(2)}, u32[]{:S(2)}) collective-permute-start(bf16[1,4096]{1,0:T(2,128)(2,1)S(1)} %get-tuple-element.198), channel_id=1, source_target_pairs={{1,0},{2,1},{3,2},{4,3},{5,4},{6,5},{7,6},{8,7},{9,8},{10,9},{11,1... | collective-permute-start | bytes 24584 | tf_op jit(solution)/shard_map/ppermute | solution.py:10
  92.3 17.2 %collective-permute-start.3 = (bf16[1,4096]{1,0:T(2,128)(2,1)S(1)}, bf16[1,4096]{1,0:T(2,128)(2,1)S(1)}, u32[]{:S(2)}, u32[]{:S(2)}) collective-permute-start(bf16[1,4096]{1,0:T(2,128)(2,1)S(1)} %get-tuple-element.197), channel_id=1, source_target_pairs={{2,0},{3,1},{4,2},{5,3},{6,4},{7,5},{8,6},{9,7},{10,8},{11,9},{12,... | collective-permute-start | bytes 24584 | tf_op jit(solution)/shard_map/ppermute | solution.py:10
  96.6 12.9 %collective-permute-start.5 = (bf16[1,4096]{1,0:T(2,128)(2,1)S(1)}, bf16[1,4096]{1,0:T(2,128)(2,1)S(1)}, u32[]{:S(2)}, u32[]{:S(2)}) collective-permute-start(bf16[1,4096]{1,0:T(2,128)(2,1)S(1)} %get-tuple-element.196), channel_id=1, source_target_pairs={{3,0},{4,1},{5,2},{6,3},{7,4},{8,5},{9,6},{10,7},{11,8},{12,9},{13... | collective-permute-start | bytes 24584 | tf_op jit(solution)/shard_map/ppermute | solution.py:10
  115.5 207.9 %all-gather.8.cloned.1.call-start = ((), (), s32[]{:S(2)}) async-start(), calls=%async_computation.6 | async-start | bytes 1064960 | tf_op jit(solution)/shard_map/all_gather | solution.py:96
  247.4 255.4 %reduce-scatter.7.cloned.1.call-start = ((), (), s32[]{:S(2)}) async-start(), calls=%async_computation.7 | async-start | bytes 2129920 | tf_op jit(solution)/shard_map/reduce_scatter | solution.py:94
  323.4 25.9 %collective-permute-start.6 = (bf16[64,8192]{1,0:T(8,128)(2,1)}, bf16[64,8192]{1,0:T(8,128)(2,1)S(1)}, u32[]{:S(2)}, u32[]{:S(2)}) collective-permute-start(bf16[64,8192]{1,0:T(8,128)(2,1)} %all-gather.8.cloned.1.call-done), channel_id=1, source_target_pairs={{192,0},{0,64},{64,128},{128,192},{193,1},{1,65},{65,129},{129,193... | collective-permute-start | bytes 3145736 | tf_op jit(solution)/shard_map/ppermute | solution.py:10
  355.2 6.5 collective-permute-start.7
  370.7 208.7 %all-gather.10.cloned.1.call-start = ((), (), s32[]{:S(2)}) async-start(), calls=%async_computation.8 | async-start | bytes 1064960 | tf_op jit(solution)/shard_map/all_gather | solution.py:96
  504.2 254.6 %reduce-scatter.9.cloned.1.call-start = ((), (), s32[]{:S(2)}) async-start(), calls=%async_computation.9 | async-start | bytes 2129920 | tf_op jit(solution)/shard_map/reduce_scatter | solution.py:94
  579.4 25.9 %collective-permute-start.10 = (bf16[64,8192]{1,0:T(8,128)(2,1)}, bf16[64,8192]{1,0:T(8,128)(2,1)S(1)}, u32[]{:S(2)}, u32[]{:S(2)}) collective-permute-start(bf16[64,8192]{1,0:T(8,128)(2,1)} %all-gather.10.cloned.1.call-done), channel_id=1, source_target_pairs={{192,0},{0,64},{64,128},{128,192},{193,1},{1,65},{65,129},{129,193... | collective-permute-start | bytes 3145736 | tf_op jit(solution)/shard_map/ppermute | solution.py:10
  611.2 6.5 collective-permute-start.11
  612.3 5.4 collective-permute-start.12
  626.7 209.2 %all-gather.12.cloned.1.call-start = ((), (), s32[]{:S(2)}) async-start(), calls=%async_computation.10 | async-start | bytes 1064960 | tf_op jit(solution)/shard_map/all_gather | solution.py:96
  760.2 255.0 %reduce-scatter.11.cloned.1.call-start = ((), (), s32[]{:S(2)}) async-start(), calls=%async_computation.11 | async-start | bytes 2129920 | tf_op jit(solution)/shard_map/reduce_scatter | solution.py:94
  835.9 25.9 %collective-permute-start.14 = (bf16[64,8192]{1,0:T(8,128)(2,1)}, bf16[64,8192]{1,0:T(8,128)(2,1)S(1)}, u32[]{:S(2)}, u32[]{:S(2)}) collective-permute-start(bf16[64,8192]{1,0:T(8,128)(2,1)} %all-gather.12.cloned.1.call-done), channel_id=1, source_target_pairs={{192,0},{0,64},{64,128},{128,192},{193,1},{1,65},{65,129},{129,193... | collective-permute-start | bytes 3145736 | tf_op jit(solution)/shard_map/ppermute | solution.py:10
  867.6 6.5 collective-permute-start.15
  868.8 5.4 collective-permute-start.16
  883.2 208.8 %all-gather.14.cloned.1.call-start = ((), (), s32[]{:S(2)}) async-start(), calls=%async_computation.12 | async-start | bytes 1064960 | tf_op jit(solution)/shard_map/all_gather | solution.py:96
  1092.0 26.0 %collective-permute-start.18 = (bf16[64,8192]{1,0:T(8,128)(2,1)}, bf16[64,8192]{1,0:T(8,128)(2,1)}, u32[]{:S(2)}, u32[]{:S(2)}) collective-permute-start(bf16[64,8192]{1,0:T(8,128)(2,1)} %all-gather.14.cloned.1.call-done), channel_id=1, source_target_pairs={{192,0},{0,64},{64,128},{128,192},{193,1},{1,65},{65,129},{129,193... | collective-permute-start | bytes 3145736 | tf_op jit(solution)/shard_map/ppermute | solution.py:10
  (15 other events, 110.3 us)
Sparse Core Ops, SparseCore 0:
  13.0 71.5 all-gather.5
  115.6 130.3 reduce-scatter.4
  248.9 74.4 all-gather.7
  370.9 131.9 reduce-scatter.6
  505.2 74.1 all-gather.9
  626.8 131.9 reduce-scatter.8
  761.7 74.1 all-gather.11
  883.3 131.9 reduce-scatter.10
  1017.8 74.1 all-gather.13
where the time goes:
time: 1130 us
  waiting for transfers between devices  976 us (86%)
  matrix products  40.5 us (4%)
  starting transfers between devices  37.1 us (3%)
  other arithmetic  25.9 us (2%)
  local copies, waits for them, and re-layouts  25.1 us (2%)
  between operations  21.4 us (2%)
    reduce_scatter x4, waiting for transfers between devices, body(): lax.psum_scatter(partial_sum, 'tp', scatter_dimension=1, tiled=True)  527 us
    all_gather x4, waiting for transfers between devices, body(): section_full = lax.all_gather(y_own, 'tp', axis=1, tiled=True)  302 us
    ppermute x19, waiting for transfers between devices, passed_along(): return lax.ppermute(block, axis, route)  108 us
    all_gather x1, waiting for transfers between devices, body(): x_full = lax.all_gather(tokens, 'tp', axis=1, tiled=True)  38.5 us
    ppermute x19, starting transfers between devices, passed_along(): return lax.ppermute(block, axis, route)  36.8 us
  transfers between devices with their start and end apart: 28, of which 16 were waited for; matrix products, arithmetic and copies ran while one was open for 3% of the time, Pallas kernels for 0%

commit v1 on v0

--- a/solution.py
+++ b/solution.py
@@ -93,7 +93,9 @@
         partial_sum = jnp.dot(mine, w_down, preferred_element_type=jnp.float32)
         summed = lax.psum_scatter(partial_sum, "tp", scatter_dimension=1, tiled=True)
         y_own = (x_own.astype(jnp.float32) + summed).astype(jnp.bfloat16)
-        section_full = lax.all_gather(y_own, "tp", axis=1, tiled=True)
+        section_full = jnp.concatenate(
+            lax.all_to_all(jnp.stack([y_own] * lax.psum(1, "tp")), "tp", 0, 0), axis=1
+        )
         x_full = passed_along(section_full, "section", 1)
         got_own = lax.dynamic_slice_in_dim(x_full, tp_pos * own_cols, own_cols, 1)
         saved = jnp.where(section_pos == (round_pos + 1) % sections, got_own, saved)

time: 1130 us -> 986 us (0.87)
  waiting for transfers between devices: 976 us -> 672 us
  blocking collectives: 0 us -> 166 us
    all_gather x4 -> x0, waiting for transfers between devices: 302 us -> none  [body(): section_full = lax.all_gather(y_own, 'tp', axis=1, tiled=True)]
    all_to_all x0 -> x4, blocking collectives: none -> 166 us  [body(): lax.all_to_all(jnp.stack([y_own] * lax.psum(1, 'tp')), 'tp', 0, 0)]
  transfers between devices with their start and end apart: 28 -> 24, of which waited for: 16 -> 12; matrix products, arithmetic and copies ran while one was open for 3% -> 4% of each run, Pallas kernels for 0% -> 0%
where the time goes in v1:
time: 986 us; the launch traced here: 977 us
  waiting for transfers between devices  672 us (68%)
  blocking collectives  166 us (17%)
  matrix products  33.6 us (3%)
  local copies, waits for them, and re-layouts  29.9 us (3%)
  starting transfers between devices  29.2 us (3%)
  other arithmetic  23.5 us (2%)
  between operations  21.8 us (2%)
    reduce_scatter x4, waiting for transfers between devices, body(): lax.psum_scatter(partial_sum, 'tp', scatter_dimension=1, tiled=True)  525 us
    all_to_all x4, blocking collectives, body(): lax.all_to_all(jnp.stack([y_own] * lax.psum(1, 'tp')), 'tp', 0, 0)  166 us
    ppermute x19, waiting for transfers between devices, passed_along(): return lax.ppermute(block, axis, route)  108 us
    all_gather x1, waiting for transfers between devices, body(): x_full = lax.all_gather(tokens, 'tp', axis=1, tiled=True)  38.5 us
    ppermute x19, starting transfers between devices, passed_along(): return lax.ppermute(block, axis, route)  29.1 us
    unnamed x31, local copies, waits for them, and re-layouts  21.5 us
  transfers between devices with their start and end apart: 24, of which 12 were waited for; matrix products, arithmetic and copies ran while one was open for 4% of the time, Pallas kernels for 0%

profile of v1, /device:TPU:1, one launch (start us, length us, event | category | flops | bytes accessed | tf_op | source)
XLA Modules:
  0.0 976.5 jit_solution(18155442855897687632)
XLA Ops:
  16.4 6.4 copy.52
  23.1 6.5 copy.53
  30.5 4.6 bitcast_multiply_fusion.2
  46.1 38.5 %all-gather.2.cloned.1.call-done = bf16[64,8192]{1,0:T(8,128)(2,1)} async-done(((bf16[64,128]{1,0:T(8,128)(2,1)}), bf16[64,8192]{1,0:T(8,128)(2,1)}) %all-gather.2.cloned.1.call-update) | async-done | bytes 1048592 | tf_op jit(solution)/shard_map/all_gather | solution.py:64
  86.2 4.1 fusion.34
  92.3 4.3 collective-permute-start.3
  98.5 6.4 copy.57
  105.0 4.4 bitcast_multiply_fusion
  110.6 4.9 fusion.6
  115.6 130.8 %reduce-scatter.5.cloned.1.call-done = f32[64,128]{1,0:T(8,128)} async-done(((f32[64,8192]{1,0:T(8,128)}), f32[64,128]{1,0:T(8,128)}) %reduce-scatter.5.cloned.1.call-update) | async-done | bytes 32784 | tf_op jit(solution)/shard_map/reduce_scatter | solution.py:94
  247.4 41.4 %all_to_all.20 = bf16[64,64,128]{2,1,0:T(8,128)(2,1)S(1)} all-to-all(bf16[64,64,128]{2,1,0:T(8,128)(2,1)S(1)} %stack.53), channel_id=1, replica_groups=mesh['section'=4,'tp'=64] {'tp'}, dimensions={0} | all-to-all | bytes 2097152 | tf_op jit(solution)/shard_map/all_to_all | solution.py:97
  290.2 24.7 %collective-permute-done.6 = bf16[64,8192]{1,0:T(8,128)(2,1)S(1)} collective-permute-done((bf16[64,8192]{1,0:T(8,128)(2,1)S(1)}, bf16[64,8192]{1,0:T(8,128)(2,1)S(1)}, u32[]{:S(2)}, u32[]{:S(2)}) %collective-permute-start.6) | collective-permute-done | bytes 1048608 | tf_op jit(solution)/shard_map/ppermute | solution.py:10
  326.9 4.9 fusion.4
  331.9 131.5 %reduce-scatter.7.cloned.1.call-done = f32[64,128]{1,0:T(8,128)} async-done(((f32[64,8192]{1,0:T(8,128)}), f32[64,128]{1,0:T(8,128)}) %reduce-scatter.7.cloned.1.call-update) | async-done | bytes 32784 | tf_op jit(solution)/shard_map/reduce_scatter | solution.py:94
  464.5 41.7 %all_to_all.21 = bf16[64,64,128]{2,1,0:T(8,128)(2,1)S(1)} all-to-all(bf16[64,64,128]{2,1,0:T(8,128)(2,1)S(1)} %stack.59), channel_id=1, replica_groups=mesh['section'=4,'tp'=64] {'tp'}, dimensions={0} | all-to-all | bytes 2097152 | tf_op jit(solution)/shard_map/all_to_all | solution.py:97
  507.6 24.7 %collective-permute-done.10 = bf16[64,8192]{1,0:T(8,128)(2,1)S(1)} collective-permute-done((bf16[64,8192]{1,0:T(8,128)(2,1)S(1)}, bf16[64,8192]{1,0:T(8,128)(2,1)S(1)}, u32[]{:S(2)}, u32[]{:S(2)}) %collective-permute-start.10) | collective-permute-done | bytes 1048608 | tf_op jit(solution)/shard_map/ppermute | solution.py:10
  544.5 4.9 fusion.2
  549.5 131.5 %reduce-scatter.9.cloned.1.call-done = f32[64,128]{1,0:T(8,128)} async-done(((f32[64,8192]{1,0:T(8,128)}), f32[64,128]{1,0:T(8,128)}) %reduce-scatter.9.cloned.1.call-update) | async-done | bytes 32784 | tf_op jit(solution)/shard_map/reduce_scatter | solution.py:94
  682.0 41.7 %all_to_all.22 = bf16[64,64,128]{2,1,0:T(8,128)(2,1)S(1)} all-to-all(bf16[64,64,128]{2,1,0:T(8,128)(2,1)S(1)} %stack.65), channel_id=1, replica_groups=mesh['section'=4,'tp'=64] {'tp'}, dimensions={0} | all-to-all | bytes 2097152 | tf_op jit(solution)/shard_map/all_to_all | solution.py:97
  725.1 24.7 %collective-permute-done.14 = bf16[64,8192]{1,0:T(8,128)(2,1)S(1)} collective-permute-done((bf16[64,8192]{1,0:T(8,128)(2,1)S(1)}, bf16[64,8192]{1,0:T(8,128)(2,1)S(1)}, u32[]{:S(2)}, u32[]{:S(2)}) %collective-permute-start.14) | collective-permute-done | bytes 1048608 | tf_op jit(solution)/shard_map/ppermute | solution.py:10
  761.8 4.9 fusion
  766.8 131.6 %reduce-scatter.11.cloned.1.call-done = f32[64,128]{1,0:T(8,128)} async-done(((f32[64,8192]{1,0:T(8,128)}), f32[64,128]{1,0:T(8,128)}) %reduce-scatter.11.cloned.1.call-update) | async-done | bytes 32784 | tf_op jit(solution)/shard_map/reduce_scatter | solution.py:94
  899.4 41.5 %all_to_all.23 = bf16[64,64,128]{2,1,0:T(8,128)(2,1)S(1)} all-to-all(bf16[64,64,128]{2,1,0:T(8,128)(2,1)S(1)} %stack.71), channel_id=1, replica_groups=mesh['section'=4,'tp'=64] {'tp'}, dimensions={0} | all-to-all | bytes 2097152 | tf_op jit(solution)/shard_map/all_to_all | solution.py:97
  943.1 25.1 %collective-permute-done.18 = bf16[64,8192]{1,0:T(8,128)(2,1)} collective-permute-done((bf16[64,8192]{1,0:T(8,128)(2,1)}, bf16[64,8192]{1,0:T(8,128)(2,1)}, u32[]{:S(2)}, u32[]{:S(2)}) %collective-permute-start.18) | collective-permute-done | bytes 1048608 | tf_op jit(solution)/shard_map/ppermute | solution.py:10
  (160 shorter events, 69.0 us)
Async XLA Ops:
  6.5 78.0 %all-gather.2.cloned.1.call-start = ((), (), s32[]{:S(2)}) async-start(), calls=%async_computation.8 | async-start | bytes 1064960 | tf_op jit(solution)/shard_map/all_gather | solution.py:64
  6.5 31.1 %collective-permute-start = (s32[4]{0:T(128)}, s32[4]{0:T(128)S(1)}, u32[]{:S(2)}, u32[]{:S(2)}) collective-permute-start(s32[4]{0:T(128)} %bitcast.195), channel_id=1, source_target_pairs={{63,0},{0,1},{1,2},{2,3},{3,4},{4,5},{5,6},{6,7},{7,8},{8,9},{9,10... | collective-permute-start | bytes 56 | tf_op jit(solution)/shard_map/ppermute | solution.py:10
  9.6 30.2 %collective-permute-start.2 = (s32[4]{0:T(128)}, s32[4]{0:T(128)S(1)}, u32[]{:S(2)}, u32[]{:S(2)}) collective-permute-start(s32[4]{0:T(128)} %bitcast.196), channel_id=1, source_target_pairs={{62,0},{63,1},{0,2},{1,3},{2,4},{3,5},{4,6},{5,7},{6,8},{7,9},{8,1... | collective-permute-start | bytes 56 | tf_op jit(solution)/shard_map/ppermute | solution.py:10
  11.2 30.7 %collective-permute-start.4 = (s32[4]{0:T(128)}, s32[4]{0:T(128)S(1)}, u32[]{:S(2)}, u32[]{:S(2)}) collective-permute-start(s32[4]{0:T(128)} %bitcast.197), channel_id=1, source_target_pairs={{61,0},{62,1},{63,2},{0,3},{1,4},{2,5},{3,6},{4,7},{5,8},{6,9},{7,... | collective-permute-start | bytes 56 | tf_op jit(solution)/shard_map/ppermute | solution.py:10
  12.9 233.4 %reduce-scatter.5.cloned.1.call-start = ((), (), s32[]{:S(2)}) async-start(), calls=%async_computation.9 | async-start | bytes 2129920 | tf_op jit(solution)/shard_map/reduce_scatter | solution.py:94
  92.0 17.5 %collective-permute-start.1 = (bf16[1,4096]{1,0:T(2,128)(2,1)S(1)}, bf16[1,4096]{1,0:T(2,128)(2,1)S(1)}, u32[]{:S(2)}, u32[]{:S(2)}) collective-permute-start(bf16[1,4096]{1,0:T(2,128)(2,1)S(1)} %get-tuple-element.198), channel_id=1, source_target_pairs={{1,0},{2,1},{3,2},{4,3},{5,4},{6,5},{7,6},{8,7},{9,8},{10,9},{11,1... | collective-permute-start | bytes 24584 | tf_op jit(solution)/shard_map/ppermute | solution.py:10
  92.3 17.2 %collective-permute-start.3 = (bf16[1,4096]{1,0:T(2,128)(2,1)S(1)}, bf16[1,4096]{1,0:T(2,128)(2,1)S(1)}, u32[]{:S(2)}, u32[]{:S(2)}) collective-permute-start(bf16[1,4096]{1,0:T(2,128)(2,1)S(1)} %get-tuple-element.197), channel_id=1, source_target_pairs={{2,0},{3,1},{4,2},{5,3},{6,4},{7,5},{8,6},{9,7},{10,8},{11,9},{12,... | collective-permute-start | bytes 24584 | tf_op jit(solution)/shard_map/ppermute | solution.py:10
  96.6 12.9 %collective-permute-start.5 = (bf16[1,4096]{1,0:T(2,128)(2,1)S(1)}, bf16[1,4096]{1,0:T(2,128)(2,1)S(1)}, u32[]{:S(2)}, u32[]{:S(2)}) collective-permute-start(bf16[1,4096]{1,0:T(2,128)(2,1)S(1)} %get-tuple-element.196), channel_id=1, source_target_pairs={{3,0},{4,1},{5,2},{6,3},{7,4},{8,5},{9,6},{10,7},{11,8},{12,9},{13... | collective-permute-start | bytes 24584 | tf_op jit(solution)/shard_map/ppermute | solution.py:10
  115.5 348.0 %reduce-scatter.7.cloned.1.call-start = ((), (), s32[]{:S(2)}) async-start(), calls=%async_computation.10 | async-start | bytes 2129920 | tf_op jit(solution)/shard_map/reduce_scatter | solution.py:94
  288.9 26.0 %collective-permute-start.6 = (bf16[64,8192]{1,0:T(8,128)(2,1)S(1)}, bf16[64,8192]{1,0:T(8,128)(2,1)S(1)}, u32[]{:S(2)}, u32[]{:S(2)}) collective-permute-start(bf16[64,8192]{1,0:T(8,128)(2,1)S(1)} %copy_bitcast_fusion.3), channel_id=1, source_target_pairs={{192,0},{0,64},{64,128},{128,192},{193,1},{1,65},{65,129},{129,193... | collective-permute-start | bytes 3145736 | tf_op jit(solution)/shard_map/ppermute | solution.py:10
  319.2 3.7 collective-permute-start.7
  320.1 2.7 collective-permute-start.8
  321.8 4.1 collective-permute-start.9
  331.9 349.1 %reduce-scatter.9.cloned.1.call-start = ((), (), s32[]{:S(2)}) async-start(), calls=%async_computation.11 | async-start | bytes 2129920 | tf_op jit(solution)/shard_map/reduce_scatter | solution.py:94
  506.3 26.0 %collective-permute-start.10 = (bf16[64,8192]{1,0:T(8,128)(2,1)S(1)}, bf16[64,8192]{1,0:T(8,128)(2,1)S(1)}, u32[]{:S(2)}, u32[]{:S(2)}) collective-permute-start(bf16[64,8192]{1,0:T(8,128)(2,1)S(1)} %copy_bitcast_fusion.2), channel_id=1, source_target_pairs={{192,0},{0,64},{64,128},{128,192},{193,1},{1,65},{65,129},{129,193... | collective-permute-start | bytes 3145736 | tf_op jit(solution)/shard_map/ppermute | solution.py:10
  536.6 3.9 collective-permute-start.11
  537.7 2.7 collective-permute-start.12
  539.4 4.1 collective-permute-start.13
  549.4 348.9 %reduce-scatter.11.cloned.1.call-start = ((), (), s32[]{:S(2)}) async-start(), calls=%async_computation.12 | async-start | bytes 2129920 | tf_op jit(solution)/shard_map/reduce_scatter | solution.py:94
  723.8 26.0 %collective-permute-start.14 = (bf16[64,8192]{1,0:T(8,128)(2,1)S(1)}, bf16[64,8192]{1,0:T(8,128)(2,1)S(1)}, u32[]{:S(2)}, u32[]{:S(2)}) collective-permute-start(bf16[64,8192]{1,0:T(8,128)(2,1)S(1)} %copy_bitcast_fusion.1), channel_id=1, source_target_pairs={{192,0},{0,64},{64,128},{128,192},{193,1},{1,65},{65,129},{129,193... | collective-permute-start | bytes 3145736 | tf_op jit(solution)/shard_map/ppermute | solution.py:10
  754.1 3.7 collective-permute-start.15
  755.0 2.7 collective-permute-start.16
  756.7 4.1 collective-permute-start.17
  942.0 26.3 %collective-permute-start.18 = (bf16[64,8192]{1,0:T(8,128)(2,1)}, bf16[64,8192]{1,0:T(8,128)(2,1)}, u32[]{:S(2)}, u32[]{:S(2)}) collective-permute-start(bf16[64,8192]{1,0:T(8,128)(2,1)} %copy_bitcast_fusion), channel_id=1, source_target_pairs={{192,0},{0,64},{64,128},{128,192},{193,1},{1,65},{65,129},{129,193... | collective-permute-start | bytes 3145736 | tf_op jit(solution)/shard_map/ppermute | solution.py:10
  (14 other events, 292.2 us)
Sparse Core Ops, SparseCore 0:
  13.0 71.5 all-gather.1
  115.6 130.6 reduce-scatter.4
  332.0 131.4 reduce-scatter.6
  549.6 131.3 reduce-scatter.8
  766.9 131.4 reduce-scatter.10
